TPU v7x, 128 devices: a whole 4x4x4 slice. The times are simulated.
128 devices in a mesh: kgrp: 4 (over z), vpair: 32 (over x, y, core).
Axes of the slice: x: 4, y: 4, z: 4, core: 2. Of those that a mesh axis runs over, the one named last changes fastest.
Arguments:
- amplitudes: bfloat16 [64, 2, 256, 4096], P('kgrp', None, None, 'vpair'), may hold values from -6 to 6
- ladder: bfloat16 [64, 2, 256, 256], P('kgrp'), may hold values from -0.25 to 0.25
- cycle: bfloat16 [4, 3, 2, 1024, 1024], P('kgrp'), may hold values from -0.078125 to 0.078125
- partner: int32 [64, 3], P('kgrp'), may hold values from 0 to 15
- occ_energy: float32 [64, 16], P('kgrp'), may hold values from -2 to -0.5
- vir_energy: float32 [64, 64], P('kgrp'), may hold values from 0.5 to 2.5
Outputs:
- updated: bfloat16 [64, 2, 256, 4096], P('kgrp', None, None, 'vpair')
Inputs may be any that keep to these rules, and one draw needn't show every extreme that they name: The place of the partner block among the 16 blocks of its k-block group.
All inputs are finite; a program needn't handle non-finite values.
Results may differ from a plain program's by a relative error of at most 0.0049.
Values may be sent and summed in bfloat16 or wider, within the bound.
A program may use at most 192 MiB of HBM per device.

v0:
```python
import jax
import jax.numpy as jnp
from jax import lax
from jax.experimental import pallas as pl
from jax.experimental.pallas import tpu as pltpu
from jax.sharding import PartitionSpec as P

F32 = jnp.float32
BF16 = jnp.bfloat16
NT = (((1,), (1,)), ((), ()))
MESH = pl.DeviceIdType.MESH
RANKS = 32


def permutation(ref, swapped):
    def block(step, _):
        row = lax.broadcasted_iota(jnp.int32, (64, 1024), 0) + step * 64
        col = lax.broadcasted_iota(jnp.int32, (64, 1024), 1)
        x, r, n, y = row >> 9, (row >> 4) & 31, (row >> 1) & 7, row & 1
        if swapped:
            x, y = y, x
        target = n * 128 + x * 64 + r * 2 + y
        ref[pl.ds(pl.multiple_of(step * 64, 64), 64), :] = jnp.where(col == target, 1.0, 0.0).astype(BF16)
        return 0

    lax.fori_loop(0, 16, block, 0)


def kernel(
    t_hbm,
    l_hbm,
    w_hbm,
    partner,
    occ,
    vir,
    vir_rows,
    out,
    t_ref,
    l_ref,
    w_ref,
    one,
    two,
    dcat,
    send1,
    x_ref,
    strips_even,
    strips_odd,
    low_even,
    low_odd,
    high_even,
    high_odd,
    picked,
    total,
    scale,
    regroup,
    send2,
    y_ref,
    load_sem,
    send1_sem,
    recv1_sem,
    shift_send_sem,
    shift_recv_sem,
    send2_sem,
    recv2_sem,
):
    group = lax.axis_index("kgrp")
    me = lax.axis_index("vpair")
    above, below = lax.rem(group + 1, 4), lax.rem(group + 3, 4)
    strips, low_ref, high_ref = (strips_even, strips_odd), (low_even, low_odd), (high_even, high_odd)

    loads = []
    for half in range(2):
        span = pl.ds(half * 8, 8)
        loads.append(
            (
                pltpu.make_async_copy(t_hbm.at[span], t_ref.at[span], load_sem.at[2 * half]),
                pltpu.make_async_copy(l_hbm.at[span], l_ref.at[span], load_sem.at[2 * half + 1]),
            )
        )
    w_load = pltpu.make_async_copy(w_hbm, w_ref, load_sem.at[4])
    for pair in loads:
        for copy in pair:
            copy.start()
    w_load.start()

    barrier = pltpu.get_barrier_semaphore()

    def greet(i, _):
        pl.semaphore_signal(barrier, inc=1, device_id=(group, lax.rem(me + i, RANKS)), device_id_type=MESH)
        return 0

    lax.fori_loop(1, RANKS, greet, 0)
    for other in (above, below):
        pl.semaphore_signal(barrier, inc=1, device_id=(other, me), device_id_type=MESH)

    mine = pl.ds(pl.multiple_of(me * 16, 16), 16)

    def spread(source, target, send_sem, recv_sem):
        def one_peer(i, _):
            peer = lax.rem(me + i, RANKS)
            pltpu.make_async_remote_copy(
                src_ref=source.at[:, :, pl.ds(pl.multiple_of(peer * 16, 16), 16), :],
                dst_ref=target.at[:, :, mine, :],
                send_sem=send_sem,
                recv_sem=recv_sem,
                device_id=(group, peer),
                device_id_type=MESH,
            ).start()
            return 0

        lax.fori_loop(1, RANKS, one_peer, 0)

    def await_peers(ref, sem):
        part = ref.at[:, :, pl.ds(0, 16 * (RANKS - 1)), :]
        pltpu.make_async_copy(part, part, sem).wait()

    def dress(half):
        def per_block(place, _):
            n = half * 8 + place
            weights = jnp.concatenate((t_ref[n, 0], t_ref[n, 1]), axis=1)
            real = jnp.dot(l_ref[n, 0], weights, preferred_element_type=F32)
            imag = jnp.dot(l_ref[n, 1], weights, preferred_element_type=F32)
            lanes = pl.ds(pl.multiple_of(place * 128, 128), 128)
            parts = (real[:, :128] - imag[:, 128:], real[:, 128:] + imag[:, :128])
            for p in range(2):
                four = parts[p].astype(BF16).reshape(8, 2, 16, 128)
                for low in range(2):
                    dcat[p, half, pl.ds(low * 128, 128), lanes] = four[:, low].reshape(128, 128)
            return 0

        lax.fori_loop(0, 8, per_block, 0)

    def spread_dressed(parity, half):
        for p in range(2):
            for part in range(2):
                moved = lax.dot_general(
                    one[pl.ds(parity * 512 + part * 256, 256), :],
                    dcat[p, half],
                    NT,
                    preferred_element_type=F32,
                ).astype(BF16)
                for low in range(2):
                    send1[parity, half, p, low, pl.ds(part * 256, 256), :] = moved[:, low * 128 : (low + 1) * 128]
        x_ref[parity, half, :, :, mine, :] = send1[parity, half, :, :, mine, :]
        spread(send1.at[parity, half], x_ref.at[parity, half], send1_sem.at[parity, half], recv1_sem.at[parity, half])

    def shifts(parity, half):
        piece = strips[parity].at[pl.ds(half * 8, 8)]
        return [
            pltpu.make_async_remote_copy(
                src_ref=piece,
                dst_ref=target[parity].at[pl.ds(half * 8, 8)],
                send_sem=shift_send_sem.at[way, parity, half],
                recv_sem=shift_recv_sem.at[way, parity, half],
                device_id=(other, me),
                device_id_type=MESH,
            )
            for way, (target, other) in enumerate(((low_ref, above), (high_ref, below)))
        ]

    def make_strips(parity, half):
        await_peers(x_ref.at[parity, half], recv1_sem.at[parity, half])
        rows = jnp.concatenate([x_ref[parity, half, p].reshape(1024, 128).T for p in range(2)], axis=0)
        moved = jnp.dot(rows, two[...], preferred_element_type=F32).astype(BF16)
        for place in range(8):
            for p in range(2):
                for k in range(8):
                    strips[parity][half * 8 + place, p, :, pl.ds(k * 128, 128)] = moved[
                        p * 128 + k * 16 : p * 128 + (k + 1) * 16, place * 128 : (place + 1) * 128
                    ]
        for copy in shifts(parity, half):
            copy.start()

    def make_scale(parity):
        def per_block(n, _):
            row = lax.broadcasted_iota(jnp.int32, (16, 128), 0)
            lane = lax.broadcasted_iota(jnp.int32, (16, 128), 1)
            own = vir[n, 2 * me + parity]
            per_row = jnp.zeros((16, 128), F32)
            for j in range(16):
                per_row = jnp.where(row == j, own - occ[n, j], per_row)
            both = vir_rows[pl.ds(n, 1), :]
            both = jnp.broadcast_to(jnp.concatenate((both, both), axis=1), (16, 128))
            rows = pl.ds(pl.multiple_of(n * 16, 16), 16)
            for pair in range(8):
                per_lane = both - jnp.where(lane < 64, occ[n, 2 * pair], occ[n, 2 * pair + 1])
                scale[rows, pl.ds(pair * 128, 128)] = 1.0 / (per_row + per_lane)
            return 0

        lax.fori_loop(0, 16, per_block, 0)

    def pick(parity, q, source):
        def per_block(n, _):
            which = partner[n, q]
            real = source[parity][which, 0]
            imag = source[parity][which, 1]
            near = pl.ds(pl.multiple_of(n * 16, 16), 16)
            far = pl.ds(pl.multiple_of(n * 16 + 256, 16), 16)
            picked[q, 0, near, :] = real
            picked[q, 0, far, :] = imag
            picked[q, 1, near, :] = -imag
            picked[q, 1, far, :] = real
            return 0

        lax.fori_loop(0, 16, per_block, 0)

    def own_cycle(parity):
        pick(parity, 0, strips)

        def columns(step, _):
            span = pl.ds(pl.multiple_of(step * 256, 256), 256)
            some = jnp.dot(picked[0, 0], w_ref[0, 0, :, span], preferred_element_type=F32)
            some += jnp.dot(picked[0, 1], w_ref[0, 1, :, span], preferred_element_type=F32)
            for p in range(2):
                total[pl.ds(p * 256, 256), span] = some[p * 256 : (p + 1) * 256] + strips[parity][
                    :, p, :, span
                ].reshape(256, 256).astype(F32)
            return 0

        lax.fori_loop(0, 4, columns, 0)
        make_scale(parity)

    def far_cycle(parity):
        for half in range(2):
            for copy in shifts(parity, half):
                copy.wait_recv()
        pick(parity, 1, low_ref)
        pick(parity, 2, high_ref)

        def columns(step, _):
            span = pl.ds(pl.multiple_of(step * 256, 256), 256)
            some = total[:, span]
            for q in (1, 2):
                for part in range(2):
                    some += jnp.dot(picked[q, part], w_ref[q, part, :, span], preferred_element_type=F32)
            for p in range(2):
                result = (some[p * 256 : (p + 1) * 256] * scale[:, span]).astype(BF16)
                for n in range(16):
                    half, place = n // 8, n % 8
                    for pair in range(2):
                        rows = pl.ds(pl.multiple_of(half * 128 + step * 32 + pair * 16, 16), 16)
                        regroup[p, rows, pl.ds(place * 128, 128)] = result[
                            n * 16 : (n + 1) * 16, pair * 128 : (pair + 1) * 128
                        ]
            return 0

        lax.fori_loop(0, 4, columns, 0)
        for p in range(2):
            for part in range(4):
                moved = lax.dot_general(
                    two[pl.ds(part * 256, 256), :], regroup[p], NT, preferred_element_type=F32
                ).astype(BF16)
                for half in range(2):
                    send2[parity, p, half, part // 2, pl.ds((part % 2) * 256, 256), :] = moved[
                        :, half * 128 : (half + 1) * 128
                    ]
            y_ref[parity, p, :, :, mine, :] = send2[parity, p, :, :, mine, :]
            spread(send2.at[parity, p], y_ref.at[parity, p], send2_sem.at[parity, p], recv2_sem.at[parity, p])

    def finish(parity, p):
        await_peers(y_ref.at[parity, p], recv2_sem.at[parity, p])
        for half in range(2):
            rows = jnp.concatenate([y_ref[parity, p, half, low].T for low in range(2)], axis=0)
            moved = jnp.dot(rows, one[pl.ds(parity * 512, 512), :], preferred_element_type=F32).astype(BF16)
            for place in range(8):
                for low in range(2):
                    for i in range(8):
                        where = (half * 8 + place, p, pl.ds((i * 2 + low) * 16, 16))
                        tile = moved[
                            low * 128 + i * 16 : low * 128 + (i + 1) * 16, place * 128 : (place + 1) * 128
                        ]
                        if parity == 0:
                            out[where] = tile
                        else:
                            out[where] = out[where] + tile

    permutation(one, True)
    for copy in loads[0]:
        copy.wait()
    dress(0)
    pl.semaphore_wait(barrier, RANKS + 1)
    spread_dressed(0, 0)
    for copy in loads[1]:
        copy.wait()
    dress(1)
    spread_dressed(0, 1)
    spread_dressed(1, 0)
    spread_dressed(1, 1)
    permutation(two, False)
    make_strips(0, 0)
    make_strips(0, 1)
    w_load.wait()
    own_cycle(0)
    make_strips(1, 0)
    make_strips(1, 1)
    far_cycle(0)
    own_cycle(1)
    far_cycle(1)
    for parity in range(2):
        for p in range(2):
            finish(parity, p)
    for parity in range(2):
        for half in range(2):
            await_peers(send1.at[parity, half], send1_sem.at[parity, half])
            await_peers(send2.at[parity, half], send2_sem.at[parity, half])
            for copy in shifts(parity, half):
                copy.wait_send()


def per_device(amplitudes, ladder, cycle, partner, occ_energy, vir_energy):
    hbm = pl.BlockSpec(memory_space=pl.ANY)
    smem = pl.BlockSpec(memory_space=pltpu.SMEM)
    vmem = pl.BlockSpec(memory_space=pltpu.VMEM)
    exchanged = pltpu.VMEM((2, 2, 2, 2, 512, 128), BF16)
    field = pltpu.VMEM((16, 2, 16, 1024), BF16)
    square = pltpu.VMEM((1024, 1024), BF16)
    dma = pltpu.SemaphoreType.DMA
    return pl.pallas_call(
        kernel,
        out_shape=jax.ShapeDtypeStruct((16, 2, 256, 128), BF16),
        in_specs=[hbm, hbm, hbm, smem, smem, smem, vmem],
        out_specs=vmem,
        scratch_shapes=[
            pltpu.VMEM((16, 2, 256, 128), BF16),
            pltpu.VMEM((16, 2, 256, 256), BF16),
            pltpu.VMEM((3, 2, 1024, 1024), BF16),
            square,
            square,
            pltpu.VMEM((2, 2, 256, 1024), BF16),
            exchanged,
            exchanged,
            field,
            field,
            field,
            field,
            field,
            field,
            pltpu.VMEM((3, 2, 512, 1024), BF16),
            pltpu.VMEM((512, 1024), F32),
            pltpu.VMEM((256, 1024), F32),
            pltpu.VMEM((2, 256, 1024), BF16),
            exchanged,
            exchanged,
            dma((5,)),
            dma((2, 2)),
            dma((2, 2)),
            dma((2, 2, 2)),
            dma((2, 2, 2)),
            dma((2, 2)),
            dma((2, 2)),
        ],
        compiler_params=pltpu.CompilerParams(
            collective_id=0, has_side_effects=True, vmem_limit_bytes=60 * 1024 * 1024
        ),
    )(amplitudes, ladder, cycle[0], partner, occ_energy, vir_energy, vir_energy)


def solution(mesh):
    return jax.shard_map(
        per_device,
        mesh=mesh,
        in_specs=(
            P("kgrp", None, None, "vpair"),
            P("kgrp", None, None, None),
            P("kgrp", None, None, None, None),
            P("kgrp", None),
            P("kgrp", None),
            P("kgrp", None),
        ),
        out_specs=P("kgrp", None, None, "vpair"),
        check_vma=False,
    )
```

profile of v0, /device:TPU:1, one launch (start us, length us, event | category | flops | bytes accessed | tf_op | source)
XLA Modules:
  0.0 96.6 jit_solution(2657981329769003672)
XLA Ops:
  0.0 1.4 %copy.7.partner = s32[16,3]{1,0:T(8,128)} copy(s32[16,3]{0,1:T(4,128)} %param.9) | data formatting | bytes 384 | tf_op args[3]
  1.4 92.1 %shard_map.64 = bf16[16,2,256,128]{3,2,1,0:T(8,128)(2,1)} custom-call(bf16[16,2,256,128]{3,2,1,0:T(8,128)(2,1)} %t_hbm.1, bf16[16,2,256,256]{3,2,1,0:T(8,128)(2,1)} %l_hbm.1, bf16[3,2,1024,1024]{3,2,1,0:T(8,128)(2,1)} %bitcast.1, s32[16,3]{1,0:T(8,128)} %copy.7.partner, f32[16,16]{1,0:T(8,128)} %occ.1, f32[16,64]{1,0:T(8,128)} %vir_rows.1, f32[16,64]{1,0:T(8,128)} %vir_rows.1), custom_call_target="tpu_custom_call" | custom-call | tf_op jit(solution)/shard_map/pallas_call | solution.py:318
  93.5 3.1 %copy.9 = bf16[16,2,256,128]{3,2,1,0:T(8,128)(2,1)} copy(bf16[16,2,256,128]{3,2,1,0:T(8,128)(2,1)} %shard_map.64) | data formatting | bytes 4194304
where the time goes:
time: 97.3 us; the launch traced here: 96.6 us
  Pallas kernels  92.1 us (95%)
  local copies, waits for them, and re-layouts  4.49 us (5%)
    pallas_call x1, Pallas kernels, per_device(): pl.pallas_call(kernel, out_shape=jax.ShapeDtypeStruct((16, 2, 256, 128),...  92.1 us
    unnamed x2, local copies, waits for them, and re-layouts  4.49 us

commit v1 on v0

v1 whole, which is shorter than its diff:
```python
import jax
import jax.numpy as jnp
from jax import lax
from jax.experimental import pallas as pl
from jax.experimental.pallas import tpu as pltpu
from jax.sharding import PartitionSpec as P

F32 = jnp.float32
BF16 = jnp.bfloat16
NT = (((1,), (1,)), ((), ()))
MESH = pl.DeviceIdType.MESH
RANKS = 32


def permutation(ref, swapped):
    def block(step, _):
        row = lax.broadcasted_iota(jnp.int32, (64, 1024), 0) + step * 64
        col = lax.broadcasted_iota(jnp.int32, (64, 1024), 1)
        x, r, n, y = row >> 9, (row >> 4) & 31, (row >> 1) & 7, row & 1
        if swapped:
            x, y = y, x
        target = n * 128 + x * 64 + r * 2 + y
        ref[pl.ds(pl.multiple_of(step * 64, 64), 64), :] = jnp.where(col == target, 1.0, 0.0).astype(BF16)
        return 0

    lax.fori_loop(0, 16, block, 0)


def kernel(
    t_hbm,
    l_hbm,
    w_hbm,
    partner,
    occ,
    vir,
    vir_rows,
    out,
    t_ref,
    l_ref,
    w_ref,
    one,
    two,
    dcat,
    send1,
    x_ref,
    *rest,
):
    strips, low_ref, high_ref = rest[:4], rest[4:8], rest[8:12]
    (
        picked,
        total,
        scale,
        regroup,
        send2,
        y_ref,
        load_sem,
        send1_sem,
        recv1_sem,
        shift_send_sem,
        shift_recv_sem,
        send2_sem,
        recv2_sem,
    ) = rest[12:]
    group = lax.axis_index("kgrp")
    me = lax.axis_index("vpair")
    above, below = lax.rem(group + 1, 4), lax.rem(group + 3, 4)

    loads = []
    for half in range(2):
        span = pl.ds(half * 8, 8)
        loads.append(
            (
                pltpu.make_async_copy(t_hbm.at[span], t_ref.at[span], load_sem.at[2 * half]),
                pltpu.make_async_copy(l_hbm.at[span], l_ref.at[span], load_sem.at[2 * half + 1]),
            )
        )
    w_load = pltpu.make_async_copy(w_hbm, w_ref, load_sem.at[4])
    for pair in loads:
        for copy in pair:
            copy.start()
    w_load.start()

    barrier = pltpu.get_barrier_semaphore()

    def greet(i, _):
        pl.semaphore_signal(barrier, inc=1, device_id=(group, lax.rem(me + i, RANKS)), device_id_type=MESH)
        return 0

    lax.fori_loop(1, RANKS, greet, 0)
    for other in (above, below):
        pl.semaphore_signal(barrier, inc=1, device_id=(other, me), device_id_type=MESH)

    mine = pl.ds(pl.multiple_of(me * 16, 16), 16)

    def spread(source, target, send_sem, recv_sem):
        def one_peer(i, _):
            peer = lax.rem(me + i, RANKS)
            pltpu.make_async_remote_copy(
                src_ref=source.at[:, :, pl.ds(pl.multiple_of(peer * 16, 16), 16), :],
                dst_ref=target.at[:, :, mine, :],
                send_sem=send_sem,
                recv_sem=recv_sem,
                device_id=(group, peer),
                device_id_type=MESH,
            ).start()
            return 0

        lax.fori_loop(1, RANKS, one_peer, 0)

    def await_peers(ref, sem):
        part = ref.at[:, :, pl.ds(0, 16 * (RANKS - 1)), :]
        pltpu.make_async_copy(part, part, sem).wait()

    def dress(half):
        def per_block(place, _):
            n = half * 8 + place
            weights = jnp.concatenate((t_ref[n, 0], t_ref[n, 1]), axis=1)
            real = jnp.dot(l_ref[n, 0], weights, preferred_element_type=F32)
            imag = jnp.dot(l_ref[n, 1], weights, preferred_element_type=F32)
            lanes = pl.ds(pl.multiple_of(place * 128, 128), 128)
            parts = (real[:, :128] - imag[:, 128:], real[:, 128:] + imag[:, :128])
            parts = [part.reshape(8, 2, 2, 8, 128) for part in parts]
            for side in range(2):
                for low in range(2):
                    both = jnp.stack([part[:, low, side] for part in parts], axis=1)
                    dcat[side, half, pl.ds(low * 128, 128), lanes] = both.reshape(128, 128).astype(BF16)
            return 0

        lax.fori_loop(0, 8, per_block, 0)

    def spread_dressed(parity, half):
        for side in range(2):
            for part in range(2):
                moved = lax.dot_general(
                    one[pl.ds(parity * 512 + part * 256, 256), :],
                    dcat[side, half],
                    NT,
                    preferred_element_type=F32,
                ).astype(BF16)
                for low in range(2):
                    send1[parity, half, side, low, pl.ds(part * 256, 256), :] = moved[:, low * 128 : (low + 1) * 128]
        x_ref[parity, half, :, :, mine, :] = send1[parity, half, :, :, mine, :]
        spread(send1.at[parity, half], x_ref.at[parity, half], send1_sem.at[parity, half], recv1_sem.at[parity, half])

    def shifts(chunk, half):
        piece = pl.ds(half * 8, 8)
        return [
            pltpu.make_async_remote_copy(
                src_ref=strips[chunk].at[piece],
                dst_ref=target[chunk].at[piece],
                send_sem=shift_send_sem.at[way, chunk, half],
                recv_sem=shift_recv_sem.at[way, chunk, half],
                device_id=(other, me),
                device_id_type=MESH,
            )
            for way, (target, other) in enumerate(((low_ref, above), (high_ref, below)))
        ]

    def start_shifts(chunk, half):
        for copy in shifts(chunk, half):
            copy.start()

    def make_strips(parity, half):
        await_peers(x_ref.at[parity, half], recv1_sem.at[parity, half])
        rows = jnp.concatenate([x_ref[parity, half, side].reshape(1024, 128).T for side in range(2)], axis=0)
        moved = jnp.dot(rows, two[...], preferred_element_type=F32).astype(BF16)
        for side in range(2):
            for place in range(8):
                for k in range(8):
                    strips[2 * parity + side][half * 8 + place, :, pl.ds(k * 128, 128)] = moved[
                        side * 128 + k * 16 : side * 128 + (k + 1) * 16, place * 128 : (place + 1) * 128
                    ]

    def make_scale(chunk):
        parity, side = chunk // 2, chunk % 2

        def per_block(n, _):
            row = lax.broadcasted_iota(jnp.int32, (8, 128), 0)
            lane = lax.broadcasted_iota(jnp.int32, (8, 128), 1)
            own = vir[n, 2 * me + parity]
            per_row = jnp.zeros((8, 128), F32)
            for j in range(8):
                per_row = jnp.where(row == j, own - occ[n, side * 8 + j], per_row)
            both = vir_rows[pl.ds(n, 1), :]
            both = jnp.broadcast_to(jnp.concatenate((both, both), axis=1), (8, 128))
            for pair in range(8):
                per_lane = both - jnp.where(lane < 64, occ[n, 2 * pair], occ[n, 2 * pair + 1])
                scale[n, :, pl.ds(pair * 128, 128)] = 1.0 / (per_row + per_lane)
            return 0

        lax.fori_loop(0, 16, per_block, 0)

    def pick(chunk, q, source):
        def per_block(n, _):
            picked[q, pl.ds(pl.multiple_of(n * 16, 16), 16), :] = source[chunk][partner[q, n]]
            return 0

        lax.fori_loop(0, 16, per_block, 0)

    def own_cycle(chunk):
        pick(chunk, 0, strips)

        def columns(step, _):
            span = pl.ds(pl.multiple_of(step * 256, 256), 256)
            for part in range(2):
                total[part, :, span] = jnp.dot(picked[0], w_ref[0, part, :, span], preferred_element_type=F32)
            return 0

        lax.fori_loop(0, 4, columns, 0)
        make_scale(chunk)

    def far_cycle(chunk):
        for half in range(2):
            for copy in shifts(chunk, half):
                copy.wait_recv()
        pick(chunk, 1, low_ref)
        pick(chunk, 2, high_ref)
        parity, side = chunk // 2, chunk % 2

        def columns(step, _):
            span = pl.ds(pl.multiple_of(step * 256, 256), 256)
            sums = []
            for part in range(2):
                some = total[part, :, span]
                for q in (1, 2):
                    some += jnp.dot(picked[q], w_ref[q, part, :, span], preferred_element_type=F32)
                sums.append(some.reshape(16, 2, 8, 256))
            by_real, by_imag = sums
            held = strips[chunk][:, :, span].astype(F32).reshape(16, 2, 8, 256)
            factor = scale[:, :, span]
            real = (held[:, 0] + (by_real[:, 0] - by_imag[:, 1])) * factor
            imag = (held[:, 1] + (by_imag[:, 0] + by_real[:, 1])) * factor
            result = jnp.stack((real, imag), axis=1).reshape(256, 256).astype(BF16)
            for n in range(16):
                half, place = n // 8, n % 8
                for pair in range(2):
                    rows = pl.ds(pl.multiple_of(half * 128 + step * 32 + pair * 16, 16), 16)
                    regroup[rows, pl.ds(place * 128, 128)] = result[
                        n * 16 : (n + 1) * 16, pair * 128 : (pair + 1) * 128
                    ]
            return 0

        lax.fori_loop(0, 4, columns, 0)
        for part in range(4):
            moved = lax.dot_general(
                two[pl.ds(part * 256, 256), :], regroup[...], NT, preferred_element_type=F32
            ).astype(BF16)
            for half in range(2):
                send2[parity, side, half, part // 2, pl.ds((part % 2) * 256, 256), :] = moved[
                    :, half * 128 : (half + 1) * 128
                ]
        y_ref[parity, side, :, :, mine, :] = send2[parity, side, :, :, mine, :]
        spread(send2.at[parity, side], y_ref.at[parity, side], send2_sem.at[parity, side], recv2_sem.at[parity, side])

    def unpacked(chunk, half):
        parity, side = chunk // 2, chunk % 2
        rows = jnp.concatenate([y_ref[parity, side, half, low].T for low in range(2)], axis=0)
        moved = jnp.dot(rows, one[pl.ds(parity * 512, 512), :], preferred_element_type=F32)
        return moved.reshape(2, 8, 2, 8, 1024)

    def finish(chunks):
        for chunk in chunks:
            where = chunk // 2, chunk % 2
            await_peers(y_ref.at[where], recv2_sem.at[where])
        for half in range(2):
            known = {chunk % 2: unpacked(chunk, half) for chunk in chunks}
            for place in range(8):
                for low in range(2):
                    for i in range(8):
                        for p in range(2):
                            tiles = [
                                known[side][low, i, p, :, place * 128 : (place + 1) * 128]
                                if side in known
                                else jnp.zeros((8, 128), F32)
                                for side in range(2)
                            ]
                            tile = jnp.concatenate(tiles, axis=0).astype(BF16)
                            spot = (half * 8 + place, p, pl.ds((i * 2 + low) * 16, 16))
                            out[spot] = tile if chunks[0] < 2 else out[spot] + tile

    permutation(one, True)
    for copy in loads[0]:
        copy.wait()
    dress(0)
    pl.semaphore_wait(barrier, RANKS + 1)
    spread_dressed(0, 0)
    for copy in loads[1]:
        copy.wait()
    dress(1)
    spread_dressed(0, 1)
    spread_dressed(1, 0)
    spread_dressed(1, 1)
    permutation(two, False)
    make_strips(0, 0)
    start_shifts(0, 0)
    make_strips(0, 1)
    start_shifts(0, 1)
    start_shifts(1, 0)
    start_shifts(1, 1)
    w_load.wait()
    own_cycle(0)
    make_strips(1, 0)
    make_strips(1, 1)
    for chunk in (2, 3):
        for half in range(2):
            start_shifts(chunk, half)
    far_cycle(0)
    own_cycle(1)
    far_cycle(1)
    own_cycle(2)
    far_cycle(2)
    own_cycle(3)
    finish((0, 1))
    far_cycle(3)
    finish((2,))
    finish((3,))
    for first in range(2):
        for second in range(2):
            await_peers(send1.at[first, second], send1_sem.at[first, second])
            await_peers(send2.at[first, second], send2_sem.at[first, second])
    for chunk in range(4):
        for half in range(2):
            for copy in shifts(chunk, half):
                copy.wait_send()


def per_device(amplitudes, ladder, cycle, partner, occ_energy, vir_energy):
    hbm = pl.BlockSpec(memory_space=pl.ANY)
    smem = pl.BlockSpec(memory_space=pltpu.SMEM)
    vmem = pl.BlockSpec(memory_space=pltpu.VMEM)
    exchanged = pltpu.VMEM((2, 2, 2, 2, 512, 128), BF16)
    field = pltpu.VMEM((16, 16, 1024), BF16)
    square = pltpu.VMEM((1024, 1024), BF16)
    dma = pltpu.SemaphoreType.DMA
    return pl.pallas_call(
        kernel,
        out_shape=jax.ShapeDtypeStruct((16, 2, 256, 128), BF16),
        in_specs=[hbm, hbm, hbm, smem, smem, smem, vmem],
        out_specs=vmem,
        scratch_shapes=[
            pltpu.VMEM((16, 2, 256, 128), BF16),
            pltpu.VMEM((16, 2, 256, 256), BF16),
            pltpu.VMEM((3, 2, 1024, 1024), BF16),
            square,
            square,
            pltpu.VMEM((2, 2, 256, 1024), BF16),
            exchanged,
            exchanged,
            *[field] * 12,
            pltpu.VMEM((3, 256, 1024), BF16),
            pltpu.VMEM((2, 256, 1024), F32),
            pltpu.VMEM((16, 8, 1024), F32),
            pltpu.VMEM((256, 1024), BF16),
            exchanged,
            exchanged,
            dma((5,)),
            dma((2, 2)),
            dma((2, 2)),
            dma((2, 4, 2)),
            dma((2, 4, 2)),
            dma((2, 2)),
            dma((2, 2)),
        ],
        compiler_params=pltpu.CompilerParams(
            collective_id=0, has_side_effects=True, vmem_limit_bytes=60 * 1024 * 1024
        ),
    )(amplitudes, ladder, cycle[0], partner.T, occ_energy, vir_energy, vir_energy)


def solution(mesh):
    return jax.shard_map(
        per_device,
        mesh=mesh,
        in_specs=(
            P("kgrp", None, None, "vpair"),
            P("kgrp", None, None, None),
            P("kgrp", None, None, None, None),
            P("kgrp", None),
            P("kgrp", None),
            P("kgrp", None),
        ),
        out_specs=P("kgrp", None, None, "vpair"),
        check_vma=False,
    )
```

time: 97.3 us -> 88.7 us (0.912)
  Pallas kernels: 92.1 us -> 84.5 us
  local copies, waits for them, and re-layouts: 4.49 us -> 3.14 us
    pallas_call x1, Pallas kernels: 92.1 us -> 84.5 us  [per_device(): pl.pallas_call(kernel, out_shape=jax.ShapeDtypeStruct((16, 2, 256, 128),...]
    unnamed x2 -> x1, local copies, waits for them, and re-layouts: 4.49 us -> 3.14 us
where the time goes in v1:
time: 88.7 us; the launch traced here: 87.6 us
  Pallas kernels  84.5 us (95%)
  local copies, waits for them, and re-layouts  3.14 us (4%)
    pallas_call x1, Pallas kernels, per_device(): pl.pallas_call(kernel, out_shape=jax.ShapeDtypeStruct((16, 2, 256, 128),...  84.5 us
    unnamed x1, local copies, waits for them, and re-layouts  3.14 us

profile of v1, /device:TPU:1, one launch (start us, length us, event | category | flops | bytes accessed | tf_op | source)
XLA Modules:
  0.0 87.6 jit_solution(17889241941887661336)
XLA Ops:
  0.0 84.5 %shard_map.64 = bf16[16,2,256,128]{3,2,1,0:T(8,128)(2,1)} custom-call(bf16[16,2,256,128]{3,2,1,0:T(8,128)(2,1)} %t_hbm.1, bf16[16,2,256,256]{3,2,1,0:T(8,128)(2,1)} %l_hbm.1, bf16[3,2,1024,1024]{3,2,1,0:T(8,128)(2,1)} %bitcast.2, s32[3,16]{1,0:T(4,128)} %bitcast.3, f32[16,16]{1,0:T(8,128)} %occ.1, f32[16,64]{1,0:T(8,128)} %vir_rows.1, f32[16,64]{1,0:T(8,128)} %vir_rows.1), custom_call_target="tpu_custom_call" | custom-call | tf_op jit(solution)/shard_map/pallas_call | solution.py:335
  84.5 3.1 %copy.8 = bf16[16,2,256,128]{3,2,1,0:T(8,128)(2,1)} copy(bf16[16,2,256,128]{3,2,1,0:T(8,128)(2,1)} %shard_map.64) | data formatting | bytes 4194304

commit v2 on v1

--- a/solution.py
+++ b/solution.py
@@ -34,7 +34,7 @@
     occ,
     vir,
     vir_rows,
-    out,
+    out_hbm,
     t_ref,
     l_ref,
     w_ref,
@@ -51,6 +51,7 @@
         total,
         scale,
         regroup,
+        out,
         send2,
         y_ref,
         load_sem,
@@ -93,11 +94,13 @@
     mine = pl.ds(pl.multiple_of(me * 16, 16), 16)
 
     def spread(source, target, send_sem, recv_sem):
+        ahead = (slice(None),) * (len(source.shape) - 2)
+
         def one_peer(i, _):
             peer = lax.rem(me + i, RANKS)
             pltpu.make_async_remote_copy(
-                src_ref=source.at[:, :, pl.ds(pl.multiple_of(peer * 16, 16), 16), :],
-                dst_ref=target.at[:, :, mine, :],
+                src_ref=source.at[(*ahead, pl.ds(pl.multiple_of(peer * 16, 16), 16), slice(None))],
+                dst_ref=target.at[(*ahead, mine, slice(None))],
                 send_sem=send_sem,
                 recv_sem=recv_sem,
                 device_id=(group, peer),
@@ -108,7 +111,8 @@
         lax.fori_loop(1, RANKS, one_peer, 0)
 
     def await_peers(ref, sem):
-        part = ref.at[:, :, pl.ds(0, 16 * (RANKS - 1)), :]
+        ahead = (slice(None),) * (len(ref.shape) - 2)
+        part = ref.at[(*ahead, pl.ds(0, 16 * (RANKS - 1)), slice(None))]
         pltpu.make_async_copy(part, part, sem).wait()
 
     def dress(half):
@@ -128,7 +132,7 @@
 
         lax.fori_loop(0, 8, per_block, 0)
 
-    def spread_dressed(parity, half):
+    def arrange(parity, half):
         for side in range(2):
             for part in range(2):
                 moved = lax.dot_general(
@@ -140,7 +144,12 @@
                 for low in range(2):
                     send1[parity, half, side, low, pl.ds(part * 256, 256), :] = moved[:, low * 128 : (low + 1) * 128]
         x_ref[parity, half, :, :, mine, :] = send1[parity, half, :, :, mine, :]
-        spread(send1.at[parity, half], x_ref.at[parity, half], send1_sem.at[parity, half], recv1_sem.at[parity, half])
+
+    def spread_dressed(*where):
+        spread(send1.at[where], x_ref.at[where], send1_sem.at[where], recv1_sem.at[where])
+
+    def await_dressed(*where):
+        await_peers(x_ref.at[where], recv1_sem.at[where])
 
     def shifts(chunk, half):
         piece = pl.ds(half * 8, 8)
@@ -160,15 +169,14 @@
         for copy in shifts(chunk, half):
             copy.start()
 
-    def make_strips(parity, half):
-        await_peers(x_ref.at[parity, half], recv1_sem.at[parity, half])
-        rows = jnp.concatenate([x_ref[parity, half, side].reshape(1024, 128).T for side in range(2)], axis=0)
+    def make_strips(parity, half, sides):
+        rows = jnp.concatenate([x_ref[parity, half, side].reshape(1024, 128).T for side in sides], axis=0)
         moved = jnp.dot(rows, two[...], preferred_element_type=F32).astype(BF16)
-        for side in range(2):
+        for at, side in enumerate(sides):
             for place in range(8):
                 for k in range(8):
                     strips[2 * parity + side][half * 8 + place, :, pl.ds(k * 128, 128)] = moved[
-                        side * 128 + k * 16 : side * 128 + (k + 1) * 16, place * 128 : (place + 1) * 128
+                        at * 128 + k * 16 : at * 128 + (k + 1) * 16, place * 128 : (place + 1) * 128
                     ]
 
     def make_scale(chunk):
@@ -258,6 +266,10 @@
         moved = jnp.dot(rows, one[pl.ds(parity * 512, 512), :], preferred_element_type=F32)
         return moved.reshape(2, 8, 2, 8, 1024)
 
+    def store(half):
+        span = pl.ds(half * 8, 8)
+        return pltpu.make_async_copy(out.at[span], out_hbm.at[span], load_sem.at[5 + half])
+
     def finish(chunks):
         for chunk in chunks:
             where = chunk // 2, chunk % 2
@@ -277,34 +289,53 @@
                             tile = jnp.concatenate(tiles, axis=0).astype(BF16)
                             spot = (half * 8 + place, p, pl.ds((i * 2 + low) * 16, 16))
                             out[spot] = tile if chunks[0] < 2 else out[spot] + tile
+            if 3 in chunks:
+                store(half).start()
 
     permutation(one, True)
     for copy in loads[0]:
         copy.wait()
     dress(0)
+    arrange(0, 0)
     pl.semaphore_wait(barrier, RANKS + 1)
-    spread_dressed(0, 0)
+    spread_dressed(0, 0, 0)
+    spread_dressed(0, 0, 1)
     for copy in loads[1]:
         copy.wait()
     dress(1)
-    spread_dressed(0, 1)
-    spread_dressed(1, 0)
-    spread_dressed(1, 1)
+    arrange(0, 1)
     permutation(two, False)
-    make_strips(0, 0)
+    await_dressed(0, 0, 0)
+    make_strips(0, 0, (0,))
     start_shifts(0, 0)
-    make_strips(0, 1)
+    await_dressed(0, 0, 1)
+    spread_dressed(0, 1, 0)
+    spread_dressed(0, 1, 1)
+    make_strips(0, 0, (1,))
+    start_shifts(1, 0)
+    arrange(1, 0)
+    arrange(1, 1)
+
+    def strips_both(parity, half):
+        for side in range(2):
+            await_dressed(parity, half, side)
+        if (parity, half) != (1, 1):
+            spread_dressed(1, parity, 0)
+            spread_dressed(1, parity, 1)
+        make_strips(parity, half, (0, 1))
+
+    strips_both(0, 1)
     start_shifts(0, 1)
-    start_shifts(1, 0)
     start_shifts(1, 1)
     w_load.wait()
     own_cycle(0)
-    make_strips(1, 0)
-    make_strips(1, 1)
-    for chunk in (2, 3):
-        for half in range(2):
-            start_shifts(chunk, half)
+    strips_both(1, 0)
+    start_shifts(2, 0)
     far_cycle(0)
+    strips_both(1, 1)
+    start_shifts(2, 1)
+    start_shifts(3, 0)
+    start_shifts(3, 1)
     own_cycle(1)
     far_cycle(1)
     own_cycle(2)
@@ -316,16 +347,19 @@
     finish((3,))
     for first in range(2):
         for second in range(2):
-            await_peers(send1.at[first, second], send1_sem.at[first, second])
+            for third in range(2):
+                await_peers(send1.at[first, second, third], send1_sem.at[first, second, third])
             await_peers(send2.at[first, second], send2_sem.at[first, second])
     for chunk in range(4):
         for half in range(2):
             for copy in shifts(chunk, half):
                 copy.wait_send()
+    for half in range(2):
+        store(half).wait()
 
 
 def per_device(amplitudes, ladder, cycle, partner, occ_energy, vir_energy):
-    hbm = pl.BlockSpec(memory_space=pl.ANY)
+    hbm = pl.BlockSpec(memory_space=pltpu.HBM)
     smem = pl.BlockSpec(memory_space=pltpu.SMEM)
     vmem = pl.BlockSpec(memory_space=pltpu.VMEM)
     exchanged = pltpu.VMEM((2, 2, 2, 2, 512, 128), BF16)
@@ -336,7 +370,7 @@
         kernel,
         out_shape=jax.ShapeDtypeStruct((16, 2, 256, 128), BF16),
         in_specs=[hbm, hbm, hbm, smem, smem, smem, vmem],
-        out_specs=vmem,
+        out_specs=pl.BlockSpec(memory_space=pl.ANY),
         scratch_shapes=[
             pltpu.VMEM((16, 2, 256, 128), BF16),
             pltpu.VMEM((16, 2, 256, 256), BF16),
@@ -351,11 +385,12 @@
             pltpu.VMEM((2, 256, 1024), F32),
             pltpu.VMEM((16, 8, 1024), F32),
             pltpu.VMEM((256, 1024), BF16),
+            pltpu.VMEM((16, 2, 256, 128), BF16),
             exchanged,
             exchanged,
-            dma((5,)),
-            dma((2, 2)),
-            dma((2, 2)),
+            dma((7,)),
+            dma((2, 2, 2)),
+            dma((2, 2, 2)),
             dma((2, 4, 2)),
             dma((2, 4, 2)),
             dma((2, 2)),

time: 88.7 us -> 87.4 us (0.985); the launches traced: 87.6 us -> 87.2 us
  no operation moved by 1% of the time
where the time goes in v2:
time: 87.4 us; the launch traced here: 87.2 us
  Pallas kernels  84.1 us (96%)
  local copies, waits for them, and re-layouts  3.14 us (4%)
    pallas_call x1, Pallas kernels, per_device(): pl.pallas_call(kernel, out_shape=jax.ShapeDtypeStruct((16, 2, 256, 128),...  84.1 us
    unnamed x1, local copies, waits for them, and re-layouts  3.14 us

profile of v2, /device:TPU:1, one launch (start us, length us, event | category | flops | bytes accessed | tf_op | source)
XLA Modules:
  0.0 87.2 jit_solution(14160719295396649026)
XLA Ops:
  0.0 84.1 %shard_map.64 = bf16[16,2,256,128]{3,2,1,0:T(8,128)(2,1)} custom-call(bf16[16,2,256,128]{3,2,1,0:T(8,128)(2,1)} %t_hbm.1, bf16[16,2,256,256]{3,2,1,0:T(8,128)(2,1)} %l_hbm.1, bf16[3,2,1024,1024]{3,2,1,0:T(8,128)(2,1)} %bitcast.2, s32[3,16]{1,0:T(4,128)} %bitcast.3, f32[16,16]{1,0:T(8,128)} %occ.1, f32[16,64]{1,0:T(8,128)} %vir_rows.1, f32[16,64]{1,0:T(8,128)} %vir_rows.1), custom_call_target="tpu_custom_call" | custom-call | tf_op jit(solution)/shard_map/pallas_call | solution.py:369
  84.1 3.1 %copy.8 = bf16[16,2,256,128]{3,2,1,0:T(8,128)(2,1)} copy(bf16[16,2,256,128]{3,2,1,0:T(8,128)(2,1)} %shard_map.64) | data formatting | bytes 4194304

commit v3 on v2

--- a/solution.py
+++ b/solution.py
@@ -10,6 +10,7 @@
 NT = (((1,), (1,)), ((), ()))
 MESH = pl.DeviceIdType.MESH
 RANKS = 32
+STRIDE = 1
 
 
 def permutation(ref, swapped):
@@ -30,10 +31,9 @@
     t_hbm,
     l_hbm,
     w_hbm,
-    partner,
-    occ,
-    vir,
-    vir_rows,
+    partner_hbm,
+    occ_hbm,
+    vir_hbm,
     out_hbm,
     t_ref,
     l_ref,
@@ -52,6 +52,10 @@
         scale,
         regroup,
         out,
+        partner,
+        occ,
+        vir,
+        vir_rows,
         send2,
         y_ref,
         load_sem,
@@ -66,6 +70,23 @@
     me = lax.axis_index("vpair")
     above, below = lax.rem(group + 1, 4), lax.rem(group + 3, 4)
 
+    barrier = pltpu.get_barrier_semaphore()
+    mine_x, mine_y, mine_core = me // 8, (me // 2) % 4, me % 2
+
+    def peer_of(i):
+        turn = lax.rem(i * STRIDE, RANKS)
+        x = lax.rem(mine_x + turn // 8, 4)
+        y = lax.rem(mine_y + lax.rem(turn // 2, 4), 4)
+        return x * 8 + y * 2 + lax.rem(mine_core + turn, 2)
+
+    def greet(i, _):
+        pl.semaphore_signal(barrier, inc=1, device_id=(group, peer_of(i)), device_id_type=MESH)
+        return 0
+
+    lax.fori_loop(1, RANKS, greet, 0)
+    for other in (above, below):
+        pl.semaphore_signal(barrier, inc=1, device_id=(other, me), device_id_type=MESH)
+
     loads = []
     for half in range(2):
         span = pl.ds(half * 8, 8)
@@ -75,21 +96,19 @@
                 pltpu.make_async_copy(l_hbm.at[span], l_ref.at[span], load_sem.at[2 * half + 1]),
             )
         )
+    small = [
+        pltpu.make_async_copy(source, target, load_sem.at[7 + at])
+        for at, (source, target) in enumerate(
+            ((partner_hbm, partner), (occ_hbm, occ), (vir_hbm, vir), (vir_hbm, vir_rows))
+        )
+    ]
     w_load = pltpu.make_async_copy(w_hbm, w_ref, load_sem.at[4])
     for pair in loads:
         for copy in pair:
             copy.start()
+    for copy in small:
+        copy.start()
     w_load.start()
-
-    barrier = pltpu.get_barrier_semaphore()
-
-    def greet(i, _):
-        pl.semaphore_signal(barrier, inc=1, device_id=(group, lax.rem(me + i, RANKS)), device_id_type=MESH)
-        return 0
-
-    lax.fori_loop(1, RANKS, greet, 0)
-    for other in (above, below):
-        pl.semaphore_signal(barrier, inc=1, device_id=(other, me), device_id_type=MESH)
 
     mine = pl.ds(pl.multiple_of(me * 16, 16), 16)
 
@@ -97,7 +116,7 @@
         ahead = (slice(None),) * (len(source.shape) - 2)
 
         def one_peer(i, _):
-            peer = lax.rem(me + i, RANKS)
+            peer = peer_of(i)
             pltpu.make_async_remote_copy(
                 src_ref=source.at[(*ahead, pl.ds(pl.multiple_of(peer * 16, 16), 16), slice(None))],
                 dst_ref=target.at[(*ahead, mine, slice(None))],
@@ -209,12 +228,12 @@
         pick(chunk, 0, strips)
 
         def columns(step, _):
-            span = pl.ds(pl.multiple_of(step * 256, 256), 256)
+            span = pl.ds(pl.multiple_of(step * 512, 512), 512)
             for part in range(2):
                 total[part, :, span] = jnp.dot(picked[0], w_ref[0, part, :, span], preferred_element_type=F32)
             return 0
 
-        lax.fori_loop(0, 4, columns, 0)
+        lax.fori_loop(0, 2, columns, 0)
         make_scale(chunk)
 
     def far_cycle(chunk):
@@ -224,73 +243,64 @@
         pick(chunk, 1, low_ref)
         pick(chunk, 2, high_ref)
         parity, side = chunk // 2, chunk % 2
-
-        def columns(step, _):
-            span = pl.ds(pl.multiple_of(step * 256, 256), 256)
+        for step in range(2):
+            span = pl.ds(step * 512, 512)
             sums = []
             for part in range(2):
                 some = total[part, :, span]
                 for q in (1, 2):
                     some += jnp.dot(picked[q], w_ref[q, part, :, span], preferred_element_type=F32)
-                sums.append(some.reshape(16, 2, 8, 256))
+                sums.append(some.reshape(16, 2, 8, 512))
             by_real, by_imag = sums
-            held = strips[chunk][:, :, span].astype(F32).reshape(16, 2, 8, 256)
+            held = strips[chunk][:, :, span].astype(F32).reshape(16, 2, 8, 512)
             factor = scale[:, :, span]
             real = (held[:, 0] + (by_real[:, 0] - by_imag[:, 1])) * factor
             imag = (held[:, 1] + (by_imag[:, 0] + by_real[:, 1])) * factor
-            result = jnp.stack((real, imag), axis=1).reshape(256, 256).astype(BF16)
+            result = jnp.stack((real, imag), axis=1).reshape(256, 512).astype(BF16)
             for n in range(16):
                 half, place = n // 8, n % 8
-                for pair in range(2):
-                    rows = pl.ds(pl.multiple_of(half * 128 + step * 32 + pair * 16, 16), 16)
-                    regroup[rows, pl.ds(place * 128, 128)] = result[
+                for pair in range(4):
+                    regroup[pl.ds(half * 64 + pair * 16, 16), pl.ds(place * 128, 128)] = result[
                         n * 16 : (n + 1) * 16, pair * 128 : (pair + 1) * 128
                     ]
-            return 0
-
-        lax.fori_loop(0, 4, columns, 0)
-        for part in range(4):
-            moved = lax.dot_general(
-                two[pl.ds(part * 256, 256), :], regroup[...], NT, preferred_element_type=F32
-            ).astype(BF16)
-            for half in range(2):
-                send2[parity, side, half, part // 2, pl.ds((part % 2) * 256, 256), :] = moved[
-                    :, half * 128 : (half + 1) * 128
-                ]
-        y_ref[parity, side, :, :, mine, :] = send2[parity, side, :, :, mine, :]
-        spread(send2.at[parity, side], y_ref.at[parity, side], send2_sem.at[parity, side], recv2_sem.at[parity, side])
-
-    def unpacked(chunk, half):
-        parity, side = chunk // 2, chunk % 2
-        rows = jnp.concatenate([y_ref[parity, side, half, low].T for low in range(2)], axis=0)
-        moved = jnp.dot(rows, one[pl.ds(parity * 512, 512), :], preferred_element_type=F32)
-        return moved.reshape(2, 8, 2, 8, 1024)
-
-    def store(half):
-        span = pl.ds(half * 8, 8)
-        return pltpu.make_async_copy(out.at[span], out_hbm.at[span], load_sem.at[5 + half])
+            for part in range(4):
+                send2[parity, side, step, part // 2, pl.ds((part % 2) * 256, 256), :] = lax.dot_general(
+                    two[pl.ds(part * 256, 256), :], regroup[...], NT, preferred_element_type=F32
+                ).astype(BF16)
+            where = parity, side, step
+            y_ref[(*where, slice(None), mine)] = send2[(*where, slice(None), mine)]
+            spread(send2.at[where], y_ref.at[where], send2_sem.at[where], recv2_sem.at[where])
+
+    def store(step):
+        span = pl.ds(step * 128, 128)
+        return pltpu.make_async_copy(out.at[:, :, span], out_hbm.at[:, :, span], load_sem.at[5 + step])
+
+    def unpacked(chunk, step):
+        where = chunk // 2, chunk % 2, step
+        await_peers(y_ref.at[where], recv2_sem.at[where])
+        rows = jnp.concatenate([y_ref[(*where, low)].T for low in range(2)], axis=0)
+        moved = jnp.dot(rows, one[pl.ds(where[0] * 512, 512), :], preferred_element_type=F32)
+        return moved.reshape(2, 2, 4, 2, 8, 1024)
 
     def finish(chunks):
-        for chunk in chunks:
-            where = chunk // 2, chunk % 2
-            await_peers(y_ref.at[where], recv2_sem.at[where])
-        for half in range(2):
-            known = {chunk % 2: unpacked(chunk, half) for chunk in chunks}
+        for step in range(2):
+            known = {chunk % 2: unpacked(chunk, step) for chunk in chunks}
             for place in range(8):
                 for low in range(2):
-                    for i in range(8):
-                        for p in range(2):
-                            tiles = [
-                                known[side][low, i, p, :, place * 128 : (place + 1) * 128]
-                                if side in known
-                                else jnp.zeros((8, 128), F32)
-                                for side in range(2)
-                            ]
-                            tile = jnp.concatenate(tiles, axis=0).astype(BF16)
-                            spot = (half * 8 + place, p, pl.ds((i * 2 + low) * 16, 16))
-                            out[spot] = tile if chunks[0] < 2 else out[spot] + tile
+                    for half in range(2):
+                        for i in range(4):
+                            for p in range(2):
+                                tiles = [
+                                    known[side][low, half, i, p, :, place * 128 : (place + 1) * 128]
+                                    if side in known
+                                    else jnp.zeros((8, 128), F32)
+                                    for side in range(2)
+                                ]
+                                tile = jnp.concatenate(tiles, axis=0).astype(BF16)
+                                spot = (half * 8 + place, p, pl.ds(((step * 4 + i) * 2 + low) * 16, 16))
+                                out[spot] = tile if chunks[0] < 2 else out[spot] + tile
             if 3 in chunks:
-                store(half).start()
+                store(step).start()
 
     permutation(one, True)
     for copy in loads[0]:
@@ -328,6 +338,8 @@
     start_shifts(0, 1)
     start_shifts(1, 1)
     w_load.wait()
+    for copy in small:
+        copy.wait()
     own_cycle(0)
     strips_both(1, 0)
     start_shifts(2, 0)
@@ -341,15 +353,15 @@
     own_cycle(2)
     far_cycle(2)
     own_cycle(3)
+    far_cycle(3)
     finish((0, 1))
-    far_cycle(3)
     finish((2,))
     finish((3,))
     for first in range(2):
         for second in range(2):
             for third in range(2):
                 await_peers(send1.at[first, second, third], send1_sem.at[first, second, third])
-            await_peers(send2.at[first, second], send2_sem.at[first, second])
+                await_peers(send2.at[first, second, third], send2_sem.at[first, second, third])
     for chunk in range(4):
         for half in range(2):
             for copy in shifts(chunk, half):
@@ -360,8 +372,6 @@
 
 def per_device(amplitudes, ladder, cycle, partner, occ_energy, vir_energy):
     hbm = pl.BlockSpec(memory_space=pltpu.HBM)
-    smem = pl.BlockSpec(memory_space=pltpu.SMEM)
-    vmem = pl.BlockSpec(memory_space=pltpu.VMEM)
     exchanged = pltpu.VMEM((2, 2, 2, 2, 512, 128), BF16)
     field = pltpu.VMEM((16, 16, 1024), BF16)
     square = pltpu.VMEM((1024, 1024), BF16)
@@ -369,7 +379,7 @@
     return pl.pallas_call(
         kernel,
         out_shape=jax.ShapeDtypeStruct((16, 2, 256, 128), BF16),
-        in_specs=[hbm, hbm, hbm, smem, smem, smem, vmem],
+        in_specs=[hbm] * 6,
         out_specs=pl.BlockSpec(memory_space=pl.ANY),
         scratch_shapes=[
             pltpu.VMEM((16, 2, 256, 128), BF16),
@@ -384,22 +394,26 @@
             pltpu.VMEM((3, 256, 1024), BF16),
             pltpu.VMEM((2, 256, 1024), F32),
             pltpu.VMEM((16, 8, 1024), F32),
-            pltpu.VMEM((256, 1024), BF16),
+            pltpu.VMEM((128, 1024), BF16),
             pltpu.VMEM((16, 2, 256, 128), BF16),
+            pltpu.SMEM((3, 16), jnp.int32),
+            pltpu.SMEM((16, 16), F32),
+            pltpu.SMEM((16, 64), F32),
+            pltpu.VMEM((16, 64), F32),
             exchanged,
             exchanged,
-            dma((7,)),
+            dma((11,)),
             dma((2, 2, 2)),
             dma((2, 2, 2)),
             dma((2, 4, 2)),
             dma((2, 4, 2)),
-            dma((2, 2)),
-            dma((2, 2)),
+            dma((2, 2, 2)),
+            dma((2, 2, 2)),
         ],
         compiler_params=pltpu.CompilerParams(
             collective_id=0, has_side_effects=True, vmem_limit_bytes=60 * 1024 * 1024
         ),
-    )(amplitudes, ladder, cycle[0], partner.T, occ_energy, vir_energy, vir_energy)
+    )(amplitudes, ladder, cycle[0], partner.T, occ_energy, vir_energy)
 
 
 def solution(mesh):

time: 87.4 us -> 85.8 us (0.982)
  Pallas kernels: 84.1 us -> 82.5 us
    pallas_call x1, Pallas kernels: 84.1 us -> 82.5 us  [per_device(): pl.pallas_call(kernel, out_shape=jax.ShapeDtypeStruct((16, 2, 256, 128),...]
where the time goes in v3:
time: 85.8 us; the launch traced here: 85.7 us
  Pallas kernels  82.5 us (96%)
  local copies, waits for them, and re-layouts  3.14 us (4%)
    pallas_call x1, Pallas kernels, per_device(): pl.pallas_call(kernel, out_shape=jax.ShapeDtypeStruct((16, 2, 256, 128),...  82.5 us
    unnamed x1, local copies, waits for them, and re-layouts  3.14 us

profile of v3, /device:TPU:1, one launch (start us, length us, event | category | flops | bytes accessed | tf_op | source)
XLA Modules:
  0.0 85.7 jit_solution(8699893318907260757)
XLA Ops:
  0.0 82.5 %shard_map.64 = bf16[16,2,256,128]{3,2,1,0:T(8,128)(2,1)} custom-call(bf16[16,2,256,128]{3,2,1,0:T(8,128)(2,1)} %t_hbm.1, bf16[16,2,256,256]{3,2,1,0:T(8,128)(2,1)} %l_hbm.1, bf16[3,2,1024,1024]{3,2,1,0:T(8,128)(2,1)} %bitcast.2, s32[3,16]{1,0:T(4,128)} %bitcast.3, f32[16,16]{1,0:T(8,128)} %occ_hbm.1, f32[16,64]{1,0:T(8,128)} %vir_hbm.1), custom_call_target="tpu_custom_call" | custom-call | tf_op jit(solution)/shard_map/pallas_call | solution.py:379
  82.5 3.1 %copy.8 = bf16[16,2,256,128]{3,2,1,0:T(8,128)(2,1)} copy(bf16[16,2,256,128]{3,2,1,0:T(8,128)(2,1)} %shard_map.64) | data formatting | bytes 4194304

commit v4 on v3

--- a/solution.py
+++ b/solution.py
@@ -212,7 +212,7 @@
             both = jnp.broadcast_to(jnp.concatenate((both, both), axis=1), (8, 128))
             for pair in range(8):
                 per_lane = both - jnp.where(lane < 64, occ[n, 2 * pair], occ[n, 2 * pair + 1])
-                scale[n, :, pl.ds(pair * 128, 128)] = 1.0 / (per_row + per_lane)
+                scale[side, n, :, pl.ds(pair * 128, 128)] = 1.0 / (per_row + per_lane)
             return 0
 
         lax.fori_loop(0, 16, per_block, 0)
@@ -230,7 +230,7 @@
         def columns(step, _):
             span = pl.ds(pl.multiple_of(step * 512, 512), 512)
             for part in range(2):
-                total[part, :, span] = jnp.dot(picked[0], w_ref[0, part, :, span], preferred_element_type=F32)
+                total[chunk % 2, part, :, span] = jnp.dot(picked[0], w_ref[0, part, :, span], preferred_element_type=F32)
             return 0
 
         lax.fori_loop(0, 2, columns, 0)
@@ -247,13 +247,13 @@
             span = pl.ds(step * 512, 512)
             sums = []
             for part in range(2):
-                some = total[part, :, span]
+                some = total[side, part, :, span]
                 for q in (1, 2):
                     some += jnp.dot(picked[q], w_ref[q, part, :, span], preferred_element_type=F32)
                 sums.append(some.reshape(16, 2, 8, 512))
             by_real, by_imag = sums
             held = strips[chunk][:, :, span].astype(F32).reshape(16, 2, 8, 512)
-            factor = scale[:, :, span]
+            factor = scale[side, :, :, span]
             real = (held[:, 0] + (by_real[:, 0] - by_imag[:, 1])) * factor
             imag = (held[:, 1] + (by_imag[:, 0] + by_real[:, 1])) * factor
             result = jnp.stack((real, imag), axis=1).reshape(256, 512).astype(BF16)
@@ -341,6 +341,7 @@
     for copy in small:
         copy.wait()
     own_cycle(0)
+    own_cycle(1)
     strips_both(1, 0)
     start_shifts(2, 0)
     far_cycle(0)
@@ -348,13 +349,12 @@
     start_shifts(2, 1)
     start_shifts(3, 0)
     start_shifts(3, 1)
-    own_cycle(1)
     far_cycle(1)
     own_cycle(2)
+    own_cycle(3)
     far_cycle(2)
-    own_cycle(3)
+    finish((0, 1))
     far_cycle(3)
-    finish((0, 1))
     finish((2,))
     finish((3,))
     for first in range(2):
@@ -392,8 +392,8 @@
             exchanged,
             *[field] * 12,
             pltpu.VMEM((3, 256, 1024), BF16),
-            pltpu.VMEM((2, 256, 1024), F32),
-            pltpu.VMEM((16, 8, 1024), F32),
+            pltpu.VMEM((2, 2, 256, 1024), F32),
+            pltpu.VMEM((2, 16, 8, 1024), F32),
             pltpu.VMEM((128, 1024), BF16),
             pltpu.VMEM((16, 2, 256, 128), BF16),
             pltpu.SMEM((3, 16), jnp.int32),

time: 85.8 us -> 85.8 us (level)
  no operation moved by 1% of the time
where the time goes in v4:
time: 85.8 us; the launch traced here: 85.7 us
  Pallas kernels  82.5 us (96%)
  local copies, waits for them, and re-layouts  3.14 us (4%)
    pallas_call x1, Pallas kernels, per_device(): pl.pallas_call(kernel, out_shape=jax.ShapeDtypeStruct((16, 2, 256, 128),...  82.5 us
    unnamed x1, local copies, waits for them, and re-layouts  3.14 us

profile of v4, /device:TPU:1, one launch (start us, length us, event | category | flops | bytes accessed | tf_op | source)
XLA Modules:
  0.0 85.7 jit_solution(340305636090699081)
XLA Ops:
  0.0 82.5 %shard_map.64 = bf16[16,2,256,128]{3,2,1,0:T(8,128)(2,1)} custom-call(bf16[16,2,256,128]{3,2,1,0:T(8,128)(2,1)} %t_hbm.1, bf16[16,2,256,256]{3,2,1,0:T(8,128)(2,1)} %l_hbm.1, bf16[3,2,1024,1024]{3,2,1,0:T(8,128)(2,1)} %bitcast.2, s32[3,16]{1,0:T(4,128)} %bitcast.3, f32[16,16]{1,0:T(8,128)} %occ_hbm.1, f32[16,64]{1,0:T(8,128)} %vir_hbm.1), custom_call_target="tpu_custom_call" | custom-call | tf_op jit(solution)/shard_map/pallas_call | solution.py:379
  82.6 3.1 %copy.8 = bf16[16,2,256,128]{3,2,1,0:T(8,128)(2,1)} copy(bf16[16,2,256,128]{3,2,1,0:T(8,128)(2,1)} %shard_map.64) | data formatting | bytes 4194304

commit v5 on v4

--- a/solution.py
+++ b/solution.py
@@ -11,6 +11,7 @@
 MESH = pl.DeviceIdType.MESH
 RANKS = 32
 STRIDE = 1
+CUT = 768
 
 
 def permutation(ref, swapped):
@@ -45,7 +46,7 @@
     x_ref,
     *rest,
 ):
-    strips, low_ref, high_ref = rest[:4], rest[4:8], rest[8:12]
+    strips, low_ref, high_ref = rest[:4], (*rest[4:7], rest[7:9]), (*rest[9:12], rest[12:14])
     (
         picked,
         total,
@@ -65,7 +66,7 @@
         shift_recv_sem,
         send2_sem,
         recv2_sem,
-    ) = rest[12:]
+    ) = rest[14:]
     group = lax.axis_index("kgrp")
     me = lax.axis_index("vpair")
     above, below = lax.rem(group + 1, 4), lax.rem(group + 3, 4)
@@ -171,11 +172,14 @@
         await_peers(x_ref.at[where], recv1_sem.at[where])
 
     def shifts(chunk, half):
-        piece = pl.ds(half * 8, 8)
+        if chunk == 3:
+            source = strips[3].at[:, :, pl.ds(CUT * half, CUT + half * (1024 - 2 * CUT))]
+        else:
+            source = strips[chunk].at[pl.ds(half * 8, 8)]
         return [
             pltpu.make_async_remote_copy(
-                src_ref=strips[chunk].at[piece],
-                dst_ref=target[chunk].at[piece],
+                src_ref=source,
+                dst_ref=target[3][half] if chunk == 3 else target[chunk].at[pl.ds(half * 8, 8)],
                 send_sem=shift_send_sem.at[way, chunk, half],
                 recv_sem=shift_recv_sem.at[way, chunk, half],
                 device_id=(other, me),
@@ -217,15 +221,15 @@
 
         lax.fori_loop(0, 16, per_block, 0)
 
-    def pick(chunk, q, source):
+    def pick(q, source, depth=1024):
         def per_block(n, _):
-            picked[q, pl.ds(pl.multiple_of(n * 16, 16), 16), :] = source[chunk][partner[q, n]]
+            picked[q, pl.ds(pl.multiple_of(n * 16, 16), 16), pl.ds(0, depth)] = source[partner[q, n]]
             return 0
 
         lax.fori_loop(0, 16, per_block, 0)
 
     def own_cycle(chunk):
-        pick(chunk, 0, strips)
+        pick(0, strips[chunk])
 
         def columns(step, _):
             span = pl.ds(pl.multiple_of(step * 512, 512), 512)
@@ -236,12 +240,39 @@
         lax.fori_loop(0, 2, columns, 0)
         make_scale(chunk)
 
+    def await_shifts(chunk, half):
+        for copy in shifts(chunk, half):
+            copy.wait_recv()
+
+    def last_chunk_ahead():
+        await_shifts(3, 0)
+        pick(1, low_ref[3][0], CUT)
+        pick(2, high_ref[3][0], CUT)
+
+        def columns(step, _):
+            span = pl.ds(pl.multiple_of(step * 512, 512), 512)
+            for part in range(2):
+                some = total[1, part, :, span]
+                for q in (1, 2):
+                    some += jnp.dot(
+                        picked[q, :, :CUT], w_ref[q, part, pl.ds(0, CUT), span], preferred_element_type=F32
+                    )
+                total[1, part, :, span] = some
+            return 0
+
+        lax.fori_loop(0, 2, columns, 0)
+
     def far_cycle(chunk):
-        for half in range(2):
-            for copy in shifts(chunk, half):
-                copy.wait_recv()
-        pick(chunk, 1, low_ref)
-        pick(chunk, 2, high_ref)
+        if chunk == 3:
+            start, depth = CUT, 1024 - CUT
+            sources = low_ref[3][1], high_ref[3][1]
+        else:
+            await_shifts(chunk, 0)
+            start, depth = 0, 1024
+            sources = low_ref[chunk], high_ref[chunk]
+        await_shifts(chunk, 1)
+        for q in (1, 2):
+            pick(q, sources[q - 1], depth)
         parity, side = chunk // 2, chunk % 2
         for step in range(2):
             span = pl.ds(step * 512, 512)
@@ -249,7 +280,9 @@
             for part in range(2):
                 some = total[side, part, :, span]
                 for q in (1, 2):
-                    some += jnp.dot(picked[q], w_ref[q, part, :, span], preferred_element_type=F32)
+                    some += jnp.dot(
+                        picked[q, :, :depth], w_ref[q, part, pl.ds(start, depth), span], preferred_element_type=F32
+                    )
                 sums.append(some.reshape(16, 2, 8, 512))
             by_real, by_imag = sums
             held = strips[chunk][:, :, span].astype(F32).reshape(16, 2, 8, 512)
@@ -354,6 +387,7 @@
     own_cycle(3)
     far_cycle(2)
     finish((0, 1))
+    last_chunk_ahead()
     far_cycle(3)
     finish((2,))
     finish((3,))
@@ -374,6 +408,7 @@
     hbm = pl.BlockSpec(memory_space=pltpu.HBM)
     exchanged = pltpu.VMEM((2, 2, 2, 2, 512, 128), BF16)
     field = pltpu.VMEM((16, 16, 1024), BF16)
+    split = [pltpu.VMEM((16, 16, depth), BF16) for depth in (CUT, 1024 - CUT)]
     square = pltpu.VMEM((1024, 1024), BF16)
     dma = pltpu.SemaphoreType.DMA
     return pl.pallas_call(
@@ -390,7 +425,8 @@
             pltpu.VMEM((2, 2, 256, 1024), BF16),
             exchanged,
             exchanged,
-            *[field] * 12,
+            *[field] * 4,
+            *([field] * 3 + split) * 2,
             pltpu.VMEM((3, 256, 1024), BF16),
             pltpu.VMEM((2, 2, 256, 1024), F32),
             pltpu.VMEM((2, 16, 8, 1024), F32),

time: 85.8 us -> 85.7 us (level)
  no operation moved by 1% of the time
where the time goes in v5:
time: 85.7 us; the launch traced here: 85.6 us
  Pallas kernels  82.4 us (96%)
  local copies, waits for them, and re-layouts  3.14 us (4%)
    pallas_call x1, Pallas kernels, per_device(): pl.pallas_call(kernel, out_shape=jax.ShapeDtypeStruct((16, 2, 256, 128),...  82.4 us
    unnamed x1, local copies, waits for them, and re-layouts  3.14 us

profile of v5, /device:TPU:1, one launch (start us, length us, event | category | flops | bytes accessed | tf_op | source)
XLA Modules:
  0.0 85.6 jit_solution(7964326353296192863)
XLA Ops:
  0.0 82.4 %shard_map.64 = bf16[16,2,256,128]{3,2,1,0:T(8,128)(2,1)} custom-call(bf16[16,2,256,128]{3,2,1,0:T(8,128)(2,1)} %t_hbm.1, bf16[16,2,256,256]{3,2,1,0:T(8,128)(2,1)} %l_hbm.1, bf16[3,2,1024,1024]{3,2,1,0:T(8,128)(2,1)} %bitcast.2, s32[3,16]{1,0:T(4,128)} %bitcast.3, f32[16,16]{1,0:T(8,128)} %occ_hbm.1, f32[16,64]{1,0:T(8,128)} %vir_hbm.1), custom_call_target="tpu_custom_call" | custom-call | tf_op jit(solution)/shard_map/pallas_call | solution.py:414
  82.4 3.1 %copy.8 = bf16[16,2,256,128]{3,2,1,0:T(8,128)(2,1)} copy(bf16[16,2,256,128]{3,2,1,0:T(8,128)(2,1)} %shard_map.64) | data formatting | bytes 4194304

commit v6 on v5

--- a/solution.py
+++ b/solution.py
@@ -349,10 +349,10 @@
     arrange(0, 1)
     permutation(two, False)
     await_dressed(0, 0, 0)
+    spread_dressed(0, 1, 0)
     make_strips(0, 0, (0,))
     start_shifts(0, 0)
     await_dressed(0, 0, 1)
-    spread_dressed(0, 1, 0)
     spread_dressed(0, 1, 1)
     make_strips(0, 0, (1,))
     start_shifts(1, 0)
@@ -362,9 +362,8 @@
     def strips_both(parity, half):
         for side in range(2):
             await_dressed(parity, half, side)
-        if (parity, half) != (1, 1):
-            spread_dressed(1, parity, 0)
-            spread_dressed(1, parity, 1)
+            if (parity, half) != (1, 1):
+                spread_dressed(1, parity, side)
         make_strips(parity, half, (0, 1))
 
     strips_both(0, 1)

time: 85.7 us -> 83.3 us (0.972)
  Pallas kernels: 82.4 us -> 80 us
    pallas_call x1, Pallas kernels: 82.4 us -> 80 us  [per_device(): pl.pallas_call(kernel, out_shape=jax.ShapeDtypeStruct((16, 2, 256, 128),...]
where the time goes in v6:
time: 83.3 us; the launch traced here: 83.2 us
  Pallas kernels  80 us (96%)
  local copies, waits for them, and re-layouts  3.14 us (4%)
    pallas_call x1, Pallas kernels, per_device(): pl.pallas_call(kernel, out_shape=jax.ShapeDtypeStruct((16, 2, 256, 128),...  80 us
    unnamed x1, local copies, waits for them, and re-layouts  3.14 us

profile of v6, /device:TPU:1, one launch (start us, length us, event | category | flops | bytes accessed | tf_op | source)
XLA Modules:
  0.0 83.2 jit_solution(3139010467763855971)
XLA Ops:
  0.0 80.0 %shard_map.64 = bf16[16,2,256,128]{3,2,1,0:T(8,128)(2,1)} custom-call(bf16[16,2,256,128]{3,2,1,0:T(8,128)(2,1)} %t_hbm.1, bf16[16,2,256,256]{3,2,1,0:T(8,128)(2,1)} %l_hbm.1, bf16[3,2,1024,1024]{3,2,1,0:T(8,128)(2,1)} %bitcast.2, s32[3,16]{1,0:T(4,128)} %bitcast.3, f32[16,16]{1,0:T(8,128)} %occ_hbm.1, f32[16,64]{1,0:T(8,128)} %vir_hbm.1), custom_call_target="tpu_custom_call" | custom-call | tf_op jit(solution)/shard_map/pallas_call | solution.py:413
  80.1 3.1 %copy.8 = bf16[16,2,256,128]{3,2,1,0:T(8,128)(2,1)} copy(bf16[16,2,256,128]{3,2,1,0:T(8,128)(2,1)} %shard_map.64) | data formatting | bytes 4194304

commit v7 on v6

--- a/solution.py
+++ b/solution.py
@@ -385,9 +385,9 @@
     own_cycle(2)
     own_cycle(3)
     far_cycle(2)
-    finish((0, 1))
     last_chunk_ahead()
     far_cycle(3)
+    finish((0, 1))
     finish((2,))
     finish((3,))
     for first in range(2):

time: 83.3 us -> 82.5 us (level)
  no operation moved by 1% of the time
where the time goes in v7:
time: 82.5 us; the launch traced here: 82.4 us
  Pallas kernels  79.2 us (96%)
  local copies, waits for them, and re-layouts  3.14 us (4%)
    pallas_call x1, Pallas kernels, per_device(): pl.pallas_call(kernel, out_shape=jax.ShapeDtypeStruct((16, 2, 256, 128),...  79.2 us
    unnamed x1, local copies, waits for them, and re-layouts  3.14 us

profile of v7, /device:TPU:1, one launch (start us, length us, event | category | flops | bytes accessed | tf_op | source)
XLA Modules:
  0.0 82.4 jit_solution(18289377815551117235)
XLA Ops:
  0.0 79.2 %shard_map.64 = bf16[16,2,256,128]{3,2,1,0:T(8,128)(2,1)} custom-call(bf16[16,2,256,128]{3,2,1,0:T(8,128)(2,1)} %t_hbm.1, bf16[16,2,256,256]{3,2,1,0:T(8,128)(2,1)} %l_hbm.1, bf16[3,2,1024,1024]{3,2,1,0:T(8,128)(2,1)} %bitcast.2, s32[3,16]{1,0:T(4,128)} %bitcast.3, f32[16,16]{1,0:T(8,128)} %occ_hbm.1, f32[16,64]{1,0:T(8,128)} %vir_hbm.1), custom_call_target="tpu_custom_call" | custom-call | tf_op jit(solution)/shard_map/pallas_call | solution.py:413
  79.2 3.1 %copy.8 = bf16[16,2,256,128]{3,2,1,0:T(8,128)(2,1)} copy(bf16[16,2,256,128]{3,2,1,0:T(8,128)(2,1)} %shard_map.64) | data formatting | bytes 4194304
